TPU v7x, 32 devices: a whole 2x2x4 slice. The times are simulated.
32 devices in a mesh: leaf: 8 (over z, y), rows: 4 (over x, core).
Axes of the slice: x: 2, y: 2, z: 4, core: 2. Of those that a mesh axis runs over, the one named last changes fastest.
Arguments:
- factor_zero: bfloat16 [4096, 4096], P('leaf', 'rows'), may hold values from -1 to 3, as said below
- factor_one: bfloat16 [8192, 4096], P('leaf', 'rows'), may hold values from -1 to 3, as said below
- factor_two: bfloat16 [16384, 4096], P('leaf', 'rows'), may hold values from -1 to 3, as said below
- factor_three: bfloat16 [32768, 4096], P('leaf', 'rows'), may hold values from -1 to 3, as said below
- coupling_one: bfloat16 [8192, 1, 4096], P('leaf', None, 'rows'), may hold values from -0.046875 to 0.046875
- coupling_two: bfloat16 [16384, 2, 4096], P('leaf', None, 'rows'), may hold values from -0.046875 to 0.046875
- coupling_three: bfloat16 [32768, 3, 4096], P('leaf', None, 'rows'), may hold values from -0.046875 to 0.046875
- noise_zero: bfloat16 [4096, 128], P('leaf'), may hold values from -6 to 6
- noise_one: bfloat16 [8192, 128], P('leaf'), may hold values from -6 to 6
- noise_two: bfloat16 [16384, 128], P('leaf'), may hold values from -6 to 6
- noise_three: bfloat16 [32768, 128], P('leaf'), may hold values from -6 to 6
- tail_index: int32 [16], replicated, may hold values from 0 to 127
Outputs:
- grad_zero: float32 [4096, 128], P('leaf')
- grad_one: float32 [8192, 128], P('leaf')
- grad_two: float32 [16384, 128], P('leaf')
- grad_three: float32 [32768, 128], P('leaf')
- tail_loss: float32 [], replicated
Inputs may be any that keep to these rules, and one draw needn't show every extreme that they name: `factor_zero`: each 4096 x 4096 node block is lower triangular with a positive diagonal. `factor_one`: each 4096 x 4096 node block is lower triangular with a positive diagonal. `factor_two`: each 4096 x 4096 node block is lower triangular with a positive diagonal. `factor_three`: each 4096 x 4096 node block is lower triangular with a positive diagonal.
All inputs are finite; a program needn't handle non-finite values.
Results may differ from a plain program's by a relative error of at most 0.008.
Values sent between devices are 32-bit elements; how exact they have to be, the bound alone decides.
No kernel may reach another device: no remote copies, remote signals or barrier semaphores. Data moves between devices by JAX's collectives and lax.ppermute only.
A program may use at most 192 MiB of HBM per device.

v0:
```python
import jax
import jax.numpy as jnp
from jax import lax
from jax.sharding import PartitionSpec as P

LEVELS = 4
tail_level = 0.5


def swapped(x, axis, apart):
    return lax.ppermute(x, axis, [(i, i ^ 1 << apart) for i in range(lax.axis_size(axis))])


def halve_bits(partial_value, bit_count, leaf_index):
    for position in range(bit_count):
        half_rows = partial_value.shape[0] // 2
        upper_bit = leaf_index >> position & 1
        kept_half = lax.dynamic_slice_in_dim(partial_value, upper_bit * half_rows, half_rows, 0)
        sent_half = lax.dynamic_slice_in_dim(
            partial_value, (1 - upper_bit) * half_rows, half_rows, 0
        )
        partial_value = kept_half + swapped(sent_half, "leaf", position)
    return partial_value


def double_bits(partial_value, bit_count, leaf_index):
    for position in reversed(range(bit_count)):
        partner = swapped(partial_value, "leaf", position)
        upper_bit = leaf_index >> position & 1
        partial_value = jnp.where(
            upper_bit == 1,
            jnp.concatenate([partner, partial_value], axis=0),
            jnp.concatenate([partial_value, partner], axis=0),
        )
    return partial_value


def group_sum(partial_value, group_bits, leaf_index):
    halved_bits = min(2, group_bits)
    partial_value = halve_bits(partial_value, halved_bits, leaf_index)
    for position in range(halved_bits, group_bits):
        partial_value = partial_value + swapped(partial_value, "leaf", position)
    return double_bits(partial_value, halved_bits, leaf_index)


def on_device(
    factor_zero,
    factor_one,
    factor_two,
    factor_three,
    coupling_one,
    coupling_two,
    coupling_three,
    noise_zero,
    noise_one,
    noise_two,
    noise_three,
    tail_index,
):
    factors = [factor_zero, factor_one, factor_two, factor_three]
    couplings = [None, coupling_one, coupling_two, coupling_three]
    noises = [noise_zero, noise_one, noise_two, noise_three]
    leaf_bits = lax.axis_size("leaf").bit_length() - 1
    leaf_index = lax.axis_index("leaf")
    full_width = factor_zero.shape[1] * lax.axis_size("rows")
    scenario_count = noise_zero.shape[1]
    columns = jnp.arange(scenario_count, dtype=jnp.int32)
    counts = jnp.sum((tail_index[:, None] == columns[None, :]).astype(jnp.float32), axis=0)
    weights = 1.0 + counts
    contract_rows = (((0,), (0,)), ((), ()))
    rounded = []
    cotangents = []
    loss_sum = jnp.float32(0.0)
    for tree_level in range(LEVELS):
        group_bits = leaf_bits - tree_level
        right_side = noises[tree_level].astype(jnp.float32)
        if tree_level > 0:
            coupling = couplings[tree_level]
            flat_coupling = coupling.reshape(
                coupling.shape[0], coupling.shape[1] * coupling.shape[2]
            )
            stacked = jnp.concatenate(rounded, axis=0)
            ancestor_terms = jnp.dot(flat_coupling, stacked, preferred_element_type=jnp.float32)
            right_side = right_side - lax.psum(ancestor_terms, "rows")
        right_round = right_side.astype(jnp.bfloat16)
        partial_sample = lax.dot_general(
            factors[tree_level], right_round, contract_rows, preferred_element_type=jnp.float32
        )
        sample = group_sum(partial_sample, group_bits, leaf_index)
        rounded.append(sample.astype(jnp.bfloat16))
        shifted = sample - tail_level
        cotangents.append(weights[None, :] * jax.nn.sigmoid(shifted))
        piece_rows = sample.shape[0] >> group_bits
        member = leaf_index & (1 << group_bits) - 1
        own_rows = lax.dynamic_slice_in_dim(shifted, member * piece_rows, piece_rows, 0)
        loss_sum = loss_sum + jnp.sum(weights[None, :] * jax.nn.softplus(own_rows))
    loss_total = lax.psum(loss_sum, ("leaf", "rows"))
    tail_loss = loss_total / jnp.float32(
        (2**LEVELS - 1) * full_width * (scenario_count + tail_index.shape[0])
    )
    pending = [jnp.zeros_like(cotangents[0]) for tree_level in range(LEVELS - 1)]
    gradients = [None] * LEVELS
    for tree_level in reversed(range(LEVELS)):
        group_bits = leaf_bits - tree_level
        if tree_level == LEVELS - 1:
            adjoint = cotangents[tree_level]
        else:
            adjoint = cotangents[tree_level] - group_sum(
                pending[tree_level], group_bits, leaf_index
            )
        adjoint_round = adjoint.astype(jnp.bfloat16)
        solved_terms = jnp.dot(
            factors[tree_level], adjoint_round, preferred_element_type=jnp.float32
        )
        solved_exact = lax.psum(solved_terms, "rows")
        gradients[tree_level] = solved_exact
        if tree_level > 0:
            solved = solved_exact.astype(jnp.bfloat16)
            upward = lax.dot_general(
                couplings[tree_level], solved, contract_rows, preferred_element_type=jnp.float32
            )
            for ancestor in range(tree_level):
                pending[ancestor] = pending[ancestor] + upward[ancestor]
    return (gradients[0], gradients[1], gradients[2], gradients[3], tail_loss)


def solution(mesh):
    in_specs = (
        P("leaf", "rows"),
        P("leaf", "rows"),
        P("leaf", "rows"),
        P("leaf", "rows"),
        P("leaf", None, "rows"),
        P("leaf", None, "rows"),
        P("leaf", None, "rows"),
        P("leaf", None),
        P("leaf", None),
        P("leaf", None),
        P("leaf", None),
        P(),
    )
    out_specs = (P("leaf", None), P("leaf", None), P("leaf", None), P("leaf", None), P())
    return jax.shard_map(
        on_device, mesh=mesh, in_specs=in_specs, out_specs=out_specs, check_vma=False
    )
```

profile of v0, /device:TPU:0, one launch (start us, length us, event | category | flops | bytes accessed | tf_op | source)
XLA Modules:
  0.0 573.5 jit_solution(12728967420345723945)
XLA Ops:
  12.1 6.3 %collective-permute-done = f32[512,128]{1,0:T(8,128)S(1)} collective-permute-done((f32[512,128]{1,0:T(8,128)S(1)}, f32[512,128]{1,0:T(8,128)S(1)}, u32[]{:S(2)}, u32[]{:S(2)}) %collective-permute-start) | collective-permute-done | bytes 262176 | tf_op jit(solution)/shard_map/ppermute | solution.py:11
  26.3 4.7 collective-permute-done.2
  31.7 4.3 collective-permute-done.3
  37.9 4.6 collective-permute-done.4
  46.1 34.3 %all-reduce.8.cloned.1.call-done = f32[1024,128]{0,1:T(8,128)} async-done(((f32[1024,128]{0,1:T(8,128)}), f32[1024,128]{0,1:T(8,128)}) %all-reduce.8.cloned.1.call-update) | async-done | bytes 524304 | tf_op jit(solution)/shard_map/psum | solution.py:84
  83.9 5.4 collective-permute-done.5
  91.2 3.7 collective-permute-done.6
  101.8 10.1 %copy.67 = bf16[256,8,2,1024]{3,1,2,0:T(8,128)(2,1)} copy(bf16[256,8,2,1024]{3,2,1,0:T(2,128)(2,1)} %bitcast.79) | data formatting | bytes 16777216
  112.0 7.3 %convolution_bitcast_fusion.2 = f32[2048,128]{0,1:T(8,128)} fusion(bf16[2048,2048]{1,0:T(8,128)(2,1)} %bitcast.78, bf16[1024,128]{1,0:T(8,128)(2,1)S(1)} %fusion.44, bf16[1024,128]{1,0:T(8,128)(2,1)S(1)} %fusion.45), kind=kOutput, calls=%fused_computation.4 | convolution fusion | flops 1074790400 | bytes 9961472 | tf_op jit(solution)/shard_map/dot_general | solution.py:83
  120.8 33.8 %all-reduce.10.cloned.1.call-done = f32[2048,128]{0,1:T(8,128)} async-done(((f32[2048,128]{0,1:T(8,128)}), f32[2048,128]{0,1:T(8,128)}) %all-reduce.10.cloned.1.call-update) | async-done | bytes 1048592 | tf_op jit(solution)/shard_map/psum | solution.py:84
  154.6 4.2 fusion.26
  160.5 6.4 %collective-permute-done.9 = f32[512,128]{1,0:T(8,128)S(1)} collective-permute-done((f32[512,128]{1,0:T(8,128)S(1)}, f32[512,128]{1,0:T(8,128)S(1)}, u32[]{:S(2)}, u32[]{:S(2)}) %collective-permute-start.9) | collective-permute-done | bytes 262176 | tf_op jit(solution)/shard_map/ppermute | solution.py:11
  168.2 33.4 %copy.51 = bf16[4096,3,1024]{0,2,1:T(8,128)(2,1)} copy(bf16[4096,3,1024]{2,0,1:T(8,128)(2,1)} %param.18) | data formatting | bytes 50331648 | tf_op args[6]
  202.6 12.9 %convolution_bitcast_fusion.1 = f32[4096,128]{0,1:T(8,128)} fusion(bf16[4096,3072]{0,1:T(8,128)(2,1)} %bitcast.77, bf16[1024,128]{1,0:T(8,128)(2,1)S(1)} %fusion.42, bf16[1024,128]{1,0:T(8,128)(2,1)S(1)} %fusion.44, bf16[1024,128]{1,0:T(8,128)(2,1)S(1)} %fusion.45), kind=kOutput, calls=%fused_computation.3 | convolution fusion | flops 3223584768 | bytes 28049408 | tf_op jit(solution)/shard_map/dot_general | solution.py:83
  217.2 49.7 %all-reduce.12.cloned.1.call-done = f32[4096,128]{0,1:T(8,128)} async-done(((f32[4096,128]{0,1:T(8,128)}), f32[4096,128]{0,1:T(8,128)}) %all-reduce.12.cloned.1.call-update) | async-done | bytes 2097168 | tf_op jit(solution)/shard_map/psum | solution.py:84
  266.9 7.4 %fusion.28 = (f32[]{:T(128)}, f32[1024,128]{1,0:T(8,128)S(1)}) fusion(f32[128]{0:T(128)S(1)} %broadcast_add_fusion, bf16[4096,1024]{1,0:T(8,128)(2,1)} %param.15, f32[4096,128]{0,1:T(8,128)} %all-reduce.12.cloned.1.call-done, bf16[4096,128]{0,1:T(8,128)(2,1)S(1)} %copy.44), kind=kOutput, calls=%fused_computation.32 | convolution fusion | flops 1076494336 | bytes 12059140 | tf_op jit(solution)/shard_map/dot_general | solution.py:86
  274.3 7.6 %convolution_bitcast_fusion = f32[4096,128]{0,1:T(8,128)} fusion(bf16[4096,1024]{1,0:T(8,128)(2,1)} %param.15, f32[1024,128]{1,0:T(8,128)S(1)} %get-tuple-element.21, f32[128]{0:T(128)S(1)} %broadcast_add_fusion), kind=kOutput, calls=%fused_computation.2 | convolution fusion | flops 1074397184 | bytes 11010560 | tf_op jit(solution)/shard_map/dot_general | solution.py:112
  282.3 51.3 %all-reduce.14.cloned.1.call-done = f32[4096,128]{0,1:T(8,128)} async-done(((f32[4096,128]{0,1:T(8,128)}), f32[4096,128]{0,1:T(8,128)}) %all-reduce.14.cloned.1.call-update) | async-done | bytes 2097168 | tf_op jit(solution)/shard_map/psum | solution.py:115
  333.6 16.0 %convolution_bitcast_fusion.4 = f32[3,1024,128]{2,1,0:T(8,128)} fusion(bf16[4096,3,1024]{2,0,1:T(8,128)(2,1)} %param.18, f32[4096,128]{0,1:T(8,128)} %all-reduce.14.cloned.1.call-done), kind=kOutput, calls=%fused_computation.12 | convolution fusion | flops 3221749760 | bytes 28835840 | tf_op jit(solution)/shard_map/dot_general | solution.py:119
  352.4 6.5 %collective-permute-done.11 = f32[512,128]{1,0:T(8,128)S(1)} collective-permute-done((f32[512,128]{1,0:T(8,128)S(1)}, f32[512,128]{1,0:T(8,128)S(1)}, u32[]{:S(2)}, u32[]{:S(2)}) %collective-permute-start.11) | collective-permute-done | bytes 262176 | tf_op jit(solution)/shard_map/ppermute | solution.py:11
  360.4 5.6 collective-permute-done.12
  366.1 4.9 convolution_bitcast_fusion.3
  371.0 36.6 %all-reduce.16.cloned.1.call-done = f32[2048,128]{0,1:T(8,128)} async-done(((f32[2048,128]{0,1:T(8,128)}), f32[2048,128]{0,1:T(8,128)}) %all-reduce.16.cloned.1.call-update) | async-done | bytes 1048592 | tf_op jit(solution)/shard_map/psum | solution.py:115
  407.6 7.6 %fusion.6 = f32[2,1024,128]{2,1,0:T(8,128)S(1)} fusion(bf16[2048,2,1024]{2,1,0:T(2,128)(2,1)} %param.17, f32[2048,128]{0,1:T(8,128)} %all-reduce.16.cloned.1.call-done), kind=kOutput, calls=%fused_computation.13 | convolution fusion | flops 1074003968 | bytes 10485760 | tf_op jit(solution)/shard_map/dot_general | solution.py:119
  418.3 6.4 %collective-permute-done.13 = f32[512,128]{1,0:T(8,128)S(1)} collective-permute-done((f32[512,128]{1,0:T(8,128)S(1)}, f32[512,128]{1,0:T(8,128)S(1)}, u32[]{:S(2)}, u32[]{:S(2)}) %collective-permute-start.13) | collective-permute-done | bytes 262176 | tf_op jit(solution)/shard_map/ppermute | solution.py:11
  426.0 3.7 collective-permute-done.14
  431.1 3.7 collective-permute-done.15
  436.1 5.1 collective-permute-done.16
  443.3 33.5 %all-reduce.18.cloned.1.call-done = f32[1024,128]{0,1:T(8,128)} async-done(((f32[1024,128]{0,1:T(8,128)}), f32[1024,128]{0,1:T(8,128)}) %all-reduce.18.cloned.1.call-update) | async-done | bytes 524304 | tf_op jit(solution)/shard_map/psum | solution.py:115
  481.3 5.4 collective-permute-done.17
  495.0 4.4 collective-permute-done.19
  516.8 39.7 %psum.63 = f32[]{:T(128)} all-reduce(f32[]{:T(128)S(6)} %add.189), channel_id=1, replica_groups=mesh['leaf'=8,'rows'=4] {'leaf','rows'}, use_global_device_ids=true, to_apply=%region_12.13 | all-reduce | flops 1 | bytes 8 | tf_op jit(solution)/shard_map/psum | solution.py:97
  (120 shorter events, 88.0 us)
Async XLA Ops:
  7.2 73.2 %copy-start = (bf16[1024,1024]{1,0:T(8,128)(2,1)S(1)}, bf16[1024,1024]{1,0:T(8,128)(2,1)}, u32[]{:S(2)}) copy-start(bf16[1024,1024]{1,0:T(8,128)(2,1)} %param.13) | copy-start | bytes 6291460
  7.2 73.2 %all-reduce.8.cloned.1.call-start = ((), (), s32[]{:S(2)}) async-start(), calls=%async_computation | async-start | bytes 1048576 | tf_op jit(solution)/shard_map/psum | solution.py:84
  9.1 9.3 %collective-permute-start = (f32[512,128]{1,0:T(8,128)S(1)}, f32[512,128]{1,0:T(8,128)S(1)}, u32[]{:S(2)}, u32[]{:S(2)}) collective-permute-start(f32[512,128]{1,0:T(8,128)S(1)} %constant_dynamic-slice_fusion.5), channel_id=1, source_target_pairs={{0,4},{4,0},{8,12},{12,8},{16,20},{20,16},{24,28},{28,24},{1,5},{5... | collective-permute-start | bytes 786440 | tf_op jit(solution)/shard_map/ppermute | solution.py:11
  18.5 5.0 collective-permute-start.1
  23.6 7.4 %collective-permute-start.2 = (f32[256,128]{1,0:T(8,128)S(1)}, f32[256,128]{1,0:T(8,128)S(1)}, u32[]{:S(2)}, u32[]{:S(2)}) collective-permute-start(f32[256,128]{1,0:T(8,128)S(1)} %dynamic-slice_add_fusion.5), channel_id=1, source_target_pairs={{0,16},{4,20},{8,24},{12,28},{16,0},{20,4},{24,8},{28,12},{1,17},{... | collective-permute-start | bytes 393224 | tf_op jit(solution)/shard_map/ppermute | solution.py:11
  31.0 5.0 collective-permute-start.3
  36.1 6.4 %collective-permute-start.4 = (f32[512,128]{1,0:T(8,128)S(1)}, f32[512,128]{1,0:T(8,128)S(1)}, u32[]{:S(2)}, u32[]{:S(2)}) collective-permute-start(f32[512,128]{1,0:T(8,128)S(1)} %maximum_select_fusion.6), channel_id=1, source_target_pairs={{0,4},{4,0},{8,12},{12,8},{16,20},{20,16},{24,28},{28,24},{1,5},{5... | collective-permute-start | bytes 786440 | tf_op jit(solution)/shard_map/ppermute | solution.py:11
  45.9 108.8 %all-reduce.10.cloned.1.call-start = ((), (), s32[]{:S(2)}) async-start(), calls=%async_computation.1 | async-start | bytes 2097152 | tf_op jit(solution)/shard_map/psum | solution.py:84
  82.4 6.9 %collective-permute-start.5 = (f32[512,128]{1,0:T(8,128)S(1)}, f32[512,128]{1,0:T(8,128)S(1)}, u32[]{:S(2)}, u32[]{:S(2)}) collective-permute-start(f32[512,128]{1,0:T(8,128)S(1)} %dynamic-slice_bitcast_fusion.3), channel_id=1, source_target_pairs={{0,4},{4,0},{8,12},{12,8},{16,20},{20,16},{24,28},{28,24},{1,5},{5... | collective-permute-start | bytes 786440 | tf_op jit(solution)/shard_map/ppermute | solution.py:11
  89.4 5.5 collective-permute-start.6
  94.9 5.0 collective-permute-start.7
  100.0 12.0 %collective-permute-start.8 = (f32[512,128]{1,0:T(8,128)S(1)}, f32[512,128]{1,0:T(8,128)S(1)}, u32[]{:S(2)}, u32[]{:S(2)}) collective-permute-start(f32[512,128]{1,0:T(8,128)S(1)} %maximum_select_fusion.7), channel_id=1, source_target_pairs={{0,4},{4,0},{8,12},{12,8},{16,20},{20,16},{24,28},{28,24},{1,5},{5... | collective-permute-start | bytes 786440 | tf_op jit(solution)/shard_map/ppermute | solution.py:11
  119.3 147.6 %all-reduce.12.cloned.1.call-start = ((), (), s32[]{:S(2)}) async-start(), calls=%async_computation.2 | async-start | bytes 4194304 | tf_op jit(solution)/shard_map/psum | solution.py:84
  158.9 7.9 %collective-permute-start.9 = (f32[512,128]{1,0:T(8,128)S(1)}, f32[512,128]{1,0:T(8,128)S(1)}, u32[]{:S(2)}, u32[]{:S(2)}) collective-permute-start(f32[512,128]{1,0:T(8,128)S(1)} %dynamic-slice_bitcast_fusion.2), channel_id=1, source_target_pairs={{0,4},{4,0},{8,12},{12,8},{16,20},{20,16},{24,28},{28,24},{1,5},{5... | collective-permute-start | bytes 786440 | tf_op jit(solution)/shard_map/ppermute | solution.py:11
  166.9 34.7 %copy-start.3 = (f32[512,128]{1,0:T(8,128)}, f32[512,128]{1,0:T(8,128)S(1)}, u32[]{:S(2)}) copy-start(f32[512,128]{1,0:T(8,128)S(1)} %bitcast_add_fusion.2) | copy-start | bytes 786436
  166.9 34.7 %collective-permute-start.10 = (f32[512,128]{1,0:T(8,128)S(1)}, f32[512,128]{1,0:T(8,128)}, u32[]{:S(2)}, u32[]{:S(2)}) collective-permute-start(f32[512,128]{1,0:T(8,128)S(1)} %bitcast_add_fusion.2), channel_id=1, source_target_pairs={{0,4},{4,0},{8,12},{12,8},{16,20},{20,16},{24,28},{28,24},{1,5},{5... | collective-permute-start | bytes 786440 | tf_op jit(solution)/shard_map/ppermute | solution.py:11
  215.6 118.0 %all-reduce.14.cloned.1.call-start = ((), (), s32[]{:S(2)}) async-start(), calls=%async_computation.3 | async-start | bytes 4194304 | tf_op jit(solution)/shard_map/psum | solution.py:115
  282.0 125.6 %all-reduce.16.cloned.1.call-start = ((), (), s32[]{:S(2)}) async-start(), calls=%async_computation.4 | async-start | bytes 2097152 | tf_op jit(solution)/shard_map/psum | solution.py:115
  350.8 8.0 %collective-permute-start.11 = (f32[512,128]{1,0:T(8,128)S(1)}, f32[512,128]{1,0:T(8,128)S(1)}, u32[]{:S(2)}, u32[]{:S(2)}) collective-permute-start(f32[512,128]{1,0:T(8,128)S(1)} %dynamic-slice_bitcast_fusion.1), channel_id=1, source_target_pairs={{0,4},{4,0},{8,12},{12,8},{16,20},{20,16},{24,28},{28,24},{1,5},{5... | collective-permute-start | bytes 786440 | tf_op jit(solution)/shard_map/ppermute | solution.py:11
  358.9 7.2 %collective-permute-start.12 = (f32[512,128]{1,0:T(8,128)S(1)}, f32[512,128]{1,0:T(8,128)S(1)}, u32[]{:S(2)}, u32[]{:S(2)}) collective-permute-start(f32[512,128]{1,0:T(8,128)S(1)} %bitcast_add_fusion.1), channel_id=1, source_target_pairs={{0,4},{4,0},{8,12},{12,8},{16,20},{20,16},{24,28},{28,24},{1,5},{5... | collective-permute-start | bytes 786440 | tf_op jit(solution)/shard_map/ppermute | solution.py:11
  371.0 105.8 %all-reduce.18.cloned.1.call-start = ((), (), s32[]{:S(2)}) async-start(), calls=%async_computation.5 | async-start | bytes 1048576 | tf_op jit(solution)/shard_map/psum | solution.py:115
  415.2 26.1 %copy-start.2 = (f32[512,128]{1,0:T(8,128)S(1)}, f32[512,128]{1,0:T(8,128)}, u32[]{:S(2)}) copy-start(f32[512,128]{1,0:T(8,128)} %copy-done.1) | copy-start | bytes 786436
  416.7 7.9 %collective-permute-start.13 = (f32[512,128]{1,0:T(8,128)S(1)}, f32[512,128]{1,0:T(8,128)S(1)}, u32[]{:S(2)}, u32[]{:S(2)}) collective-permute-start(f32[512,128]{1,0:T(8,128)S(1)} %dynamic-slice_bitcast_fusion), channel_id=1, source_target_pairs={{0,4},{4,0},{8,12},{12,8},{16,20},{20,16},{24,28},{28,24},{1,5},{5... | collective-permute-start | bytes 786440 | tf_op jit(solution)/shard_map/ppermute | solution.py:11
  424.7 5.0 collective-permute-start.14
  429.7 5.0 collective-permute-start.15
  434.8 6.4 %collective-permute-start.16 = (f32[512,128]{1,0:T(8,128)S(1)}, f32[512,128]{1,0:T(8,128)S(1)}, u32[]{:S(2)}, u32[]{:S(2)}) collective-permute-start(f32[512,128]{1,0:T(8,128)S(1)} %maximum_select_fusion.8), channel_id=1, source_target_pairs={{0,4},{4,0},{8,12},{12,8},{16,20},{20,16},{24,28},{28,24},{1,5},{5... | collective-permute-start | bytes 786440 | tf_op jit(solution)/shard_map/ppermute | solution.py:11
  443.0 120.7 %all-reduce.20.cloned.1.call-start = ((), (), s32[]{:S(2)}) async-start(), calls=%async_computation.6 | async-start | bytes 524288 | tf_op jit(solution)/shard_map/psum | solution.py:115
  479.7 6.9 %collective-permute-start.17 = (f32[512,128]{1,0:T(8,128)S(1)}, f32[512,128]{1,0:T(8,128)S(1)}, u32[]{:S(2)}, u32[]{:S(2)}) collective-permute-start(f32[512,128]{1,0:T(8,128)S(1)} %constant_dynamic-slice_fusion.1), channel_id=1, source_target_pairs={{0,4},{4,0},{8,12},{12,8},{16,20},{20,16},{24,28},{28,24},{1,5},{5... | collective-permute-start | bytes 786440 | tf_op jit(solution)/shard_map/ppermute | solution.py:11
  486.7 5.0 collective-permute-start.18
  491.7 7.6 %collective-permute-start.19 = (f32[256,128]{1,0:T(8,128)S(1)}, f32[256,128]{1,0:T(8,128)S(1)}, u32[]{:S(2)}, u32[]{:S(2)}) collective-permute-start(f32[256,128]{1,0:T(8,128)S(1)} %dynamic-slice_add_fusion.2), channel_id=1, source_target_pairs={{0,16},{4,20},{8,24},{12,28},{16,0},{20,4},{24,8},{28,12},{1,17},{... | collective-permute-start | bytes 393224 | tf_op jit(solution)/shard_map/ppermute | solution.py:11
  499.4 5.0 collective-permute-start.20
  505.1 6.7 %collective-permute-start.21 = (f32[512,128]{1,0:T(8,128)}, f32[512,128]{1,0:T(8,128)}, u32[]{:S(2)}, u32[]{:S(2)}) collective-permute-start(f32[512,128]{1,0:T(8,128)} %maximum_select_fusion.9), channel_id=1, source_target_pairs={{0,4},{4,0},{8,12},{12,8},{16,20},{20,16},{24,28},{28,24},{1,5},{5... | collective-permute-start | bytes 786440 | tf_op jit(solution)/shard_map/ppermute | solution.py:11
  (9 other events, 92.0 us)
Sparse Core Ops, SparseCore 0:
  46.0 34.3 all-reduce.7
  119.5 35.1 all-reduce.9
  215.7 51.1 all-reduce.11
  282.1 51.4 all-reduce.13
  371.1 36.4 all-reduce.15
  443.1 33.6 all-reduce.17
  514.9 31.7 all-reduce.19
where the time goes:
time: 575 us; the launch traced here: 573 us
  waiting for transfers between devices  329 us (57%)
  matrix products  82.6 us (14%)
  local copies, waits for them, and re-layouts  56.1 us (10%)
  blocking collectives  39.7 us (7%)
  starting transfers between devices  37.8 us (7%)
  between operations  18.8 us (3%)
  other arithmetic  9.3 us (2%)
    psum x4, waiting for transfers between devices, on_device(): solved_exact = lax.psum(solved_terms, 'rows')  121 us
    psum x3, waiting for transfers between devices, on_device(): right_side = right_side - lax.psum(ancestor_terms, 'rows')  118 us
    ppermute x22, waiting for transfers between devices, swapped(): lax.ppermute(x, axis, [(i, i ^ 1 << apart) for i in range(lax.axis_size(a...  89.8 us
    unnamed x33, local copies, waits for them, and re-layouts  54.7 us
    psum x1, blocking collectives, on_device(): loss_total = lax.psum(loss_sum, ('leaf', 'rows'))  39.7 us
    ppermute x22, starting transfers between devices, swapped(): lax.ppermute(x, axis, [(i, i ^ 1 << apart) for i in range(lax.axis_size(a...  36.9 us
    dot_general x3, matrix products, on_device(): lax.dot_general(couplings[tree_level], solved, contract_rows, preferred_e...  26.5 us
    dot_general x3, matrix products, on_device(): jnp.dot(flat_coupling, stacked, preferred_element_type=jnp.float32)  23.5 us
  transfers between devices with their start and end apart: 29, of which 26 were waited for; matrix products, arithmetic and copies ran while one was open for 10% of the time, Pallas kernels for 0%

commit v1 on v0

--- a/solution.py
+++ b/solution.py
@@ -1,3 +1,4 @@
+import functools
 import jax
 import jax.numpy as jnp
 from jax import lax
@@ -5,6 +6,14 @@
 
 LEVELS = 4
 tail_level = 0.5
+
+
+def get_roads(xs, net_axis):
+    state_now = lax.all_gather(xs, axis_name=net_axis).sum(axis=0)
+    return state_now
+
+
+compute_paths_on = functools.partial(get_roads, net_axis="rows")
 
 
 def swapped(x, axis, apart):
@@ -81,7 +90,7 @@
             )
             stacked = jnp.concatenate(rounded, axis=0)
             ancestor_terms = jnp.dot(flat_coupling, stacked, preferred_element_type=jnp.float32)
-            right_side = right_side - lax.psum(ancestor_terms, "rows")
+            right_side = right_side - compute_paths_on(ancestor_terms)
         right_round = right_side.astype(jnp.bfloat16)
         partial_sample = lax.dot_general(
             factors[tree_level], right_round, contract_rows, preferred_element_type=jnp.float32

time: 575 us -> 617 us (1.073); the launches traced: 573 us -> 607 us
  local copies, waits for them, and re-layouts: 56.1 us -> 77.9 us
  other arithmetic: 9.3 us -> 26 us
    psum x3 -> x0, waiting for transfers between devices: 118 us -> none  [on_device(): right_side = right_side - lax.psum(ancestor_terms, 'rows')]
    all_gather x0 -> x3, waiting for transfers between devices: none -> 112 us  [get_roads(): state_now = lax.all_gather(xs, axis_name=net_axis).sum(axis=0)]
    all_gather x0 -> x3, local copies, waits for them, and re-layouts: none -> 20.5 us  [get_roads(): state_now = lax.all_gather(xs, axis_name=net_axis).sum(axis=0)]
    reduce_sum x0 -> x3, other arithmetic: none -> 17.7 us  [get_roads(): state_now = lax.all_gather(xs, axis_name=net_axis).sum(axis=0)]
    unnamed x33 -> x45, local copies, waits for them, and re-layouts: 54.7 us -> 56 us
where the time goes in v1:
time: 617 us; the launch traced here: 607 us
  waiting for transfers between devices  325 us (53%)
  matrix products  81.1 us (13%)
  local copies, waits for them, and re-layouts  77.9 us (13%)
  blocking collectives  39.7 us (6%)
  starting transfers between devices  37.7 us (6%)
  other arithmetic  26 us (4%)
  between operations  19 us (3%)
    psum x4, waiting for transfers between devices, on_device(): solved_exact = lax.psum(solved_terms, 'rows')  121 us
    all_gather x3, waiting for transfers between devices, get_roads(): state_now = lax.all_gather(xs, axis_name=net_axis).sum(axis=0)  112 us
    ppermute x22, waiting for transfers between devices, swapped(): lax.ppermute(x, axis, [(i, i ^ 1 << apart) for i in range(lax.axis_size(a...  92.1 us
    unnamed x45, local copies, waits for them, and re-layouts  56 us
    psum x1, blocking collectives, on_device(): loss_total = lax.psum(loss_sum, ('leaf', 'rows'))  39.7 us
    ppermute x22, starting transfers between devices, swapped(): lax.ppermute(x, axis, [(i, i ^ 1 << apart) for i in range(lax.axis_size(a...  36.3 us
    dot_general x3, matrix products, on_device(): lax.dot_general(couplings[tree_level], solved, contract_rows, preferred_e...  26.5 us
    dot_general x3, matrix products, on_device(): jnp.dot(flat_coupling, stacked, preferred_element_type=jnp.float32)  23.5 us
  transfers between devices with their start and end apart: 29, of which 26 were waited for; matrix products, arithmetic and copies ran while one was open for 10% of the time, Pallas kernels for 0%

profile of v1, /device:TPU:0, one launch (start us, length us, event | category | flops | bytes accessed | tf_op | source)
XLA Modules:
  0.0 606.6 jit_solution(7835162208882671189)
XLA Ops:
  12.1 6.3 %collective-permute-done = f32[512,128]{1,0:T(8,128)S(1)} collective-permute-done((f32[512,128]{1,0:T(8,128)S(1)}, f32[512,128]{1,0:T(8,128)S(1)}, u32[]{:S(2)}, u32[]{:S(2)}) %collective-permute-start) | collective-permute-done | bytes 262176 | tf_op jit(solution)/shard_map/ppermute | solution.py:20
  26.3 4.7 collective-permute-done.2
  31.7 4.3 collective-permute-done.3
  37.9 4.6 collective-permute-done.4
  46.1 23.7 %all-gather.7.cloned.1.call-done = f32[4096,128]{0,1:T(8,128)} async-done(((f32[1024,128]{0,1:T(8,128)}), f32[4096,128]{0,1:T(8,128)}) %all-gather.7.cloned.1.call-update) | async-done | bytes 2097168 | tf_op jit(solution)/shard_map/all_gather | solution.py:12
  78.8 7.0 %collective-permute-done.5 = f32[512,128]{1,0:T(8,128)S(1)} collective-permute-done((f32[512,128]{1,0:T(8,128)S(1)}, f32[512,128]{1,0:T(8,128)S(1)}, u32[]{:S(2)}, u32[]{:S(2)}) %collective-permute-start.5) | collective-permute-done | bytes 262176 | tf_op jit(solution)/shard_map/ppermute | solution.py:20
  97.5 10.2 %copy.84 = bf16[256,8,2,1024]{3,1,2,0:T(8,128)(2,1)} copy(bf16[256,8,2,1024]{3,2,1,0:T(2,128)(2,1)} %bitcast.85) | data formatting | bytes 16777216
  109.1 7.3 %convolution_bitcast_fusion.2 = f32[2048,128]{0,1:T(8,128)} fusion(bf16[2048,2048]{1,0:T(8,128)(2,1)} %bitcast.84, bf16[1024,128]{1,0:T(8,128)(2,1)S(1)} %fusion.44, bf16[1024,128]{1,0:T(8,128)(2,1)S(1)} %fusion.45), kind=kOutput, calls=%fused_computation.4 | convolution fusion | flops 1074790400 | bytes 9961472 | tf_op jit(solution)/shard_map/dot_general | solution.py:92
  117.7 32.5 %all-gather.9.cloned.1.call-done = f32[8192,128]{0,1:T(8,128)} async-done(((f32[2048,128]{0,1:T(8,128)}), f32[8192,128]{0,1:T(8,128)}) %all-gather.9.cloned.1.call-update) | async-done | bytes 4194320 | tf_op jit(solution)/shard_map/all_gather | solution.py:12
  150.2 6.1 %reshape.36 = f32[4,2048,128]{1,0,2:T(4,128)} reshape(f32[8192,128]{0,1:T(8,128)} %all-gather.9.cloned.1.call-done) | data formatting | bytes 8388608 | tf_op jit(solution)/shard_map/all_gather | solution.py:12
  156.3 4.8 reduce_sum.74
  166.8 7.0 %collective-permute-done.9 = f32[512,128]{1,0:T(8,128)S(1)} collective-permute-done((f32[512,128]{1,0:T(8,128)S(1)}, f32[512,128]{1,0:T(8,128)S(1)}, u32[]{:S(2)}, u32[]{:S(2)}) %collective-permute-start.9) | collective-permute-done | bytes 262176 | tf_op jit(solution)/shard_map/ppermute | solution.py:20
  175.4 33.6 %copy.68 = bf16[4096,3,1024]{0,2,1:T(8,128)(2,1)} copy(bf16[4096,3,1024]{2,0,1:T(8,128)(2,1)} %param.18) | data formatting | bytes 50331648 | tf_op args[6]
  209.0 13.0 %convolution_bitcast_fusion.1 = f32[4096,128]{0,1:T(8,128)} fusion(bf16[4096,3072]{0,1:T(8,128)(2,1)} %bitcast.83, bf16[1024,128]{1,0:T(8,128)(2,1)S(1)} %fusion.42, bf16[1024,128]{1,0:T(8,128)(2,1)S(1)} %copy-done.2, bf16[1024,128]{1,0:T(8,128)(2,1)S(1)} %fusion.45), kind=kOutput, calls=%fused_computation.3 | convolution fusion | flops 3223584768 | bytes 28049408 | tf_op jit(solution)/shard_map/dot_general | solution.py:92
  223.9 55.7 %all-gather.11.cloned.1.call-done = f32[16384,128]{0,1:T(8,128)} async-done(((f32[4096,128]{0,1:T(8,128)}), f32[16384,128]{0,1:T(8,128)}) %all-gather.11.cloned.1.call-update) | async-done | bytes 8388624 | tf_op jit(solution)/shard_map/all_gather | solution.py:12
  279.6 10.8 %reshape.37 = f32[4,4096,128]{1,0,2:T(4,128)} reshape(f32[16384,128]{0,1:T(8,128)} %all-gather.11.cloned.1.call-done) | data formatting | bytes 16777216 | tf_op jit(solution)/shard_map/all_gather | solution.py:12
  290.3 10.0 %reduce_sum.75 = f32[4096,128]{0,1:T(8,128)} reduce(f32[4,4096,128]{1,0,2:T(4,128)} %reshape.37, f32[]{:T(128)} %constant.15.clone.1), dimensions={0}, to_apply=%region_3.4 | reduce | flops 1572864 | bytes 10485764 | tf_op jit(solution)/shard_map/reduce_sum | solution.py:12
  300.3 7.4 %fusion.28 = (f32[]{:T(128)}, f32[1024,128]{1,0:T(8,128)S(1)}) fusion(f32[128]{0:T(128)S(1)} %broadcast_add_fusion, bf16[4096,1024]{1,0:T(8,128)(2,1)} %param.15, f32[4096,128]{0,1:T(8,128)} %reduce_sum.75, bf16[4096,128]{0,1:T(8,128)(2,1)S(1)} %copy.61), kind=kOutput, calls=%fused_computation.32 | convolution fusion | flops 1076494336 | bytes 12059140 | tf_op jit(solution)/shard_map/dot_general | solution.py:95
  307.8 7.6 %convolution_bitcast_fusion = f32[4096,128]{0,1:T(8,128)} fusion(bf16[4096,1024]{1,0:T(8,128)(2,1)} %param.15, f32[1024,128]{1,0:T(8,128)S(1)} %get-tuple-element.26, f32[128]{0:T(128)S(1)} %broadcast_add_fusion), kind=kOutput, calls=%fused_computation.2 | convolution fusion | flops 1074397184 | bytes 11010560 | tf_op jit(solution)/shard_map/dot_general | solution.py:121
  315.7 51.2 %all-reduce.5.cloned.1.call-done = f32[4096,128]{0,1:T(8,128)} async-done(((f32[4096,128]{0,1:T(8,128)}), f32[4096,128]{0,1:T(8,128)}) %all-reduce.5.cloned.1.call-update) | async-done | bytes 2097168 | tf_op jit(solution)/shard_map/psum | solution.py:124
  367.0 16.0 %convolution_bitcast_fusion.4 = f32[3,1024,128]{2,1,0:T(8,128)} fusion(bf16[4096,3,1024]{2,0,1:T(8,128)(2,1)} %param.18, f32[4096,128]{0,1:T(8,128)} %all-reduce.5.cloned.1.call-done), kind=kOutput, calls=%fused_computation.12 | convolution fusion | flops 3221749760 | bytes 28835840 | tf_op jit(solution)/shard_map/dot_general | solution.py:128
  385.7 6.5 %collective-permute-done.11 = f32[512,128]{1,0:T(8,128)S(1)} collective-permute-done((f32[512,128]{1,0:T(8,128)S(1)}, f32[512,128]{1,0:T(8,128)S(1)}, u32[]{:S(2)}, u32[]{:S(2)}) %collective-permute-start.11) | collective-permute-done | bytes 262176 | tf_op jit(solution)/shard_map/ppermute | solution.py:20
  393.8 5.6 collective-permute-done.12
  399.4 4.7 convolution_bitcast_fusion.3
  404.2 36.6 %all-reduce.7.cloned.1.call-done = f32[2048,128]{0,1:T(8,128)} async-done(((f32[2048,128]{0,1:T(8,128)}), f32[2048,128]{0,1:T(8,128)}) %all-reduce.7.cloned.1.call-update) | async-done | bytes 1048592 | tf_op jit(solution)/shard_map/psum | solution.py:124
  440.7 7.6 %fusion.6 = f32[2,1024,128]{2,1,0:T(8,128)S(1)} fusion(bf16[2048,2,1024]{2,1,0:T(2,128)(2,1)} %param.17, f32[2048,128]{0,1:T(8,128)} %all-reduce.7.cloned.1.call-done), kind=kOutput, calls=%fused_computation.13 | convolution fusion | flops 1074003968 | bytes 10485760 | tf_op jit(solution)/shard_map/dot_general | solution.py:128
  451.4 6.4 %collective-permute-done.13 = f32[512,128]{1,0:T(8,128)S(1)} collective-permute-done((f32[512,128]{1,0:T(8,128)S(1)}, f32[512,128]{1,0:T(8,128)S(1)}, u32[]{:S(2)}, u32[]{:S(2)}) %collective-permute-start.13) | collective-permute-done | bytes 262176 | tf_op jit(solution)/shard_map/ppermute | solution.py:20
  469.2 5.1 collective-permute-done.16
  476.6 33.3 %all-reduce.9.cloned.1.call-done = f32[1024,128]{0,1:T(8,128)} async-done(((f32[1024,128]{0,1:T(8,128)}), f32[1024,128]{0,1:T(8,128)}) %all-reduce.9.cloned.1.call-update) | async-done | bytes 524304 | tf_op jit(solution)/shard_map/psum | solution.py:124
  514.4 5.4 collective-permute-done.17
  528.2 4.3 collective-permute-done.19
  549.8 39.7 %psum.39 = f32[]{:T(128)} all-reduce(f32[]{:T(128)S(6)} %add.183), channel_id=1, replica_groups=mesh['leaf'=8,'rows'=4] {'leaf','rows'}, use_global_device_ids=true, to_apply=%region_12.13 | all-reduce | flops 1 | bytes 8 | tf_op jit(solution)/shard_map/psum | solution.py:106
  (138 shorter events, 108.5 us)
Async XLA Ops:
  7.2 69.1 %copy-start = (bf16[1024,1024]{1,0:T(8,128)(2,1)S(1)}, bf16[1024,1024]{1,0:T(8,128)(2,1)}, u32[]{:S(2)}) copy-start(bf16[1024,1024]{1,0:T(8,128)(2,1)} %param.13) | copy-start | bytes 6291460
  7.2 62.6 %all-gather.7.cloned.1.call-start = ((), (), s32[]{:S(2)}) async-start(), calls=%async_computation.4 | async-start | bytes 2621440 | tf_op jit(solution)/shard_map/all_gather | solution.py:12
  9.1 9.3 %collective-permute-start = (f32[512,128]{1,0:T(8,128)S(1)}, f32[512,128]{1,0:T(8,128)S(1)}, u32[]{:S(2)}, u32[]{:S(2)}) collective-permute-start(f32[512,128]{1,0:T(8,128)S(1)} %constant_dynamic-slice_fusion.5), channel_id=1, source_target_pairs={{0,4},{4,0},{8,12},{12,8},{16,20},{20,16},{24,28},{28,24},{1,5},{5... | collective-permute-start | bytes 786440 | tf_op jit(solution)/shard_map/ppermute | solution.py:20
  18.5 5.0 collective-permute-start.1
  23.6 7.4 %collective-permute-start.2 = (f32[256,128]{1,0:T(8,128)S(1)}, f32[256,128]{1,0:T(8,128)S(1)}, u32[]{:S(2)}, u32[]{:S(2)}) collective-permute-start(f32[256,128]{1,0:T(8,128)S(1)} %dynamic-slice_add_fusion.5), channel_id=1, source_target_pairs={{0,16},{4,20},{8,24},{12,28},{16,0},{20,4},{24,8},{28,12},{1,17},{... | collective-permute-start | bytes 393224 | tf_op jit(solution)/shard_map/ppermute | solution.py:20
  31.0 5.0 collective-permute-start.3
  36.1 6.4 %collective-permute-start.4 = (f32[512,128]{1,0:T(8,128)S(1)}, f32[512,128]{1,0:T(8,128)S(1)}, u32[]{:S(2)}, u32[]{:S(2)}) collective-permute-start(f32[512,128]{1,0:T(8,128)S(1)} %maximum_select_fusion.6), channel_id=1, source_target_pairs={{0,4},{4,0},{8,12},{12,8},{16,20},{20,16},{24,28},{28,24},{1,5},{5... | collective-permute-start | bytes 786440 | tf_op jit(solution)/shard_map/ppermute | solution.py:20
  45.9 104.3 %all-gather.9.cloned.1.call-start = ((), (), s32[]{:S(2)}) async-start(), calls=%async_computation.5 | async-start | bytes 5242880 | tf_op jit(solution)/shard_map/all_gather | solution.py:12
  77.3 8.5 %collective-permute-start.5 = (f32[512,128]{1,0:T(8,128)S(1)}, f32[512,128]{1,0:T(8,128)S(1)}, u32[]{:S(2)}, u32[]{:S(2)}) collective-permute-start(f32[512,128]{1,0:T(8,128)S(1)} %dynamic-slice_bitcast_fusion.3), channel_id=1, source_target_pairs={{0,4},{4,0},{8,12},{12,8},{16,20},{20,16},{24,28},{28,24},{1,5},{5... | collective-permute-start | bytes 786440 | tf_op jit(solution)/shard_map/ppermute | solution.py:20
  85.8 5.0 collective-permute-start.6
  90.9 5.0 collective-permute-start.7
  96.0 11.7 %collective-permute-start.8 = (f32[512,128]{1,0:T(8,128)S(1)}, f32[512,128]{1,0:T(8,128)S(1)}, u32[]{:S(2)}, u32[]{:S(2)}) collective-permute-start(f32[512,128]{1,0:T(8,128)S(1)} %maximum_select_fusion.7), channel_id=1, source_target_pairs={{0,4},{4,0},{8,12},{12,8},{16,20},{20,16},{24,28},{28,24},{1,5},{5... | collective-permute-start | bytes 786440 | tf_op jit(solution)/shard_map/ppermute | solution.py:20
  116.5 163.1 %all-gather.11.cloned.1.call-start = ((), (), s32[]{:S(2)}) async-start(), calls=%async_computation.6 | async-start | bytes 10485760 | tf_op jit(solution)/shard_map/all_gather | solution.py:12
  165.3 8.5 %collective-permute-start.9 = (f32[512,128]{1,0:T(8,128)S(1)}, f32[512,128]{1,0:T(8,128)S(1)}, u32[]{:S(2)}, u32[]{:S(2)}) collective-permute-start(f32[512,128]{1,0:T(8,128)S(1)} %dynamic-slice_bitcast_fusion.2), channel_id=1, source_target_pairs={{0,4},{4,0},{8,12},{12,8},{16,20},{20,16},{24,28},{28,24},{1,5},{5... | collective-permute-start | bytes 786440 | tf_op jit(solution)/shard_map/ppermute | solution.py:20
  173.8 35.2 %copy-start.2 = (bf16[1024,128]{1,0:T(8,128)(2,1)S(1)}, bf16[1024,128]{1,0:T(8,128)(2,1)}, u32[]{:S(2)}) copy-start(bf16[1024,128]{1,0:T(8,128)(2,1)} %copy-done.1) | copy-start | bytes 786436
  173.9 35.1 %collective-permute-start.10 = (f32[512,128]{1,0:T(8,128)S(1)}, f32[512,128]{1,0:T(8,128)S(1)}, u32[]{:S(2)}, u32[]{:S(2)}) collective-permute-start(f32[512,128]{1,0:T(8,128)S(1)} %bitcast_add_fusion.2), channel_id=1, source_target_pairs={{0,4},{4,0},{8,12},{12,8},{16,20},{20,16},{24,28},{28,24},{1,5},{5... | collective-permute-start | bytes 786440 | tf_op jit(solution)/shard_map/ppermute | solution.py:20
  222.0 144.9 %all-reduce.5.cloned.1.call-start = ((), (), s32[]{:S(2)}) async-start(), calls=%async_computation | async-start | bytes 4194304 | tf_op jit(solution)/shard_map/psum | solution.py:124
  315.4 125.3 %all-reduce.7.cloned.1.call-start = ((), (), s32[]{:S(2)}) async-start(), calls=%async_computation.1 | async-start | bytes 2097152 | tf_op jit(solution)/shard_map/psum | solution.py:124
  384.2 8.0 %collective-permute-start.11 = (f32[512,128]{1,0:T(8,128)S(1)}, f32[512,128]{1,0:T(8,128)S(1)}, u32[]{:S(2)}, u32[]{:S(2)}) collective-permute-start(f32[512,128]{1,0:T(8,128)S(1)} %dynamic-slice_bitcast_fusion.1), channel_id=1, source_target_pairs={{0,4},{4,0},{8,12},{12,8},{16,20},{20,16},{24,28},{28,24},{1,5},{5... | collective-permute-start | bytes 786440 | tf_op jit(solution)/shard_map/ppermute | solution.py:20
  392.2 7.2 %collective-permute-start.12 = (f32[512,128]{1,0:T(8,128)S(1)}, f32[512,128]{1,0:T(8,128)S(1)}, u32[]{:S(2)}, u32[]{:S(2)}) collective-permute-start(f32[512,128]{1,0:T(8,128)S(1)} %bitcast_add_fusion.1), channel_id=1, source_target_pairs={{0,4},{4,0},{8,12},{12,8},{16,20},{20,16},{24,28},{28,24},{1,5},{5... | collective-permute-start | bytes 786440 | tf_op jit(solution)/shard_map/ppermute | solution.py:20
  404.1 105.8 %all-reduce.9.cloned.1.call-start = ((), (), s32[]{:S(2)}) async-start(), calls=%async_computation.2 | async-start | bytes 1048576 | tf_op jit(solution)/shard_map/psum | solution.py:124
  448.3 26.1 %copy-start.6 = (f32[512,128]{1,0:T(8,128)S(1)}, f32[512,128]{1,0:T(8,128)}, u32[]{:S(2)}) copy-start(f32[512,128]{1,0:T(8,128)} %copy-done.5) | copy-start | bytes 786436
  449.9 7.9 %collective-permute-start.13 = (f32[512,128]{1,0:T(8,128)S(1)}, f32[512,128]{1,0:T(8,128)S(1)}, u32[]{:S(2)}, u32[]{:S(2)}) collective-permute-start(f32[512,128]{1,0:T(8,128)S(1)} %dynamic-slice_bitcast_fusion), channel_id=1, source_target_pairs={{0,4},{4,0},{8,12},{12,8},{16,20},{20,16},{24,28},{28,24},{1,5},{5... | collective-permute-start | bytes 786440 | tf_op jit(solution)/shard_map/ppermute | solution.py:20
  457.8 5.0 collective-permute-start.14
  462.9 5.0 collective-permute-start.15
  467.9 6.4 %collective-permute-start.16 = (f32[512,128]{1,0:T(8,128)S(1)}, f32[512,128]{1,0:T(8,128)S(1)}, u32[]{:S(2)}, u32[]{:S(2)}) collective-permute-start(f32[512,128]{1,0:T(8,128)S(1)} %maximum_select_fusion.8), channel_id=1, source_target_pairs={{0,4},{4,0},{8,12},{12,8},{16,20},{20,16},{24,28},{28,24},{1,5},{5... | collective-permute-start | bytes 786440 | tf_op jit(solution)/shard_map/ppermute | solution.py:20
  476.1 120.6 %all-reduce.11.cloned.1.call-start = ((), (), s32[]{:S(2)}) async-start(), calls=%async_computation.3 | async-start | bytes 524288 | tf_op jit(solution)/shard_map/psum | solution.py:124
  512.9 6.9 %collective-permute-start.17 = (f32[512,128]{1,0:T(8,128)S(1)}, f32[512,128]{1,0:T(8,128)S(1)}, u32[]{:S(2)}, u32[]{:S(2)}) collective-permute-start(f32[512,128]{1,0:T(8,128)S(1)} %constant_dynamic-slice_fusion.1), channel_id=1, source_target_pairs={{0,4},{4,0},{8,12},{12,8},{16,20},{20,16},{24,28},{28,24},{1,5},{5... | collective-permute-start | bytes 786440 | tf_op jit(solution)/shard_map/ppermute | solution.py:20
  519.8 5.0 collective-permute-start.18
  524.9 7.6 %collective-permute-start.19 = (f32[256,128]{1,0:T(8,128)S(1)}, f32[256,128]{1,0:T(8,128)S(1)}, u32[]{:S(2)}, u32[]{:S(2)}) collective-permute-start(f32[256,128]{1,0:T(8,128)S(1)} %dynamic-slice_add_fusion.2), channel_id=1, source_target_pairs={{0,16},{4,20},{8,24},{12,28},{16,0},{20,4},{24,8},{28,12},{1,17},{... | collective-permute-start | bytes 393224 | tf_op jit(solution)/shard_map/ppermute | solution.py:20
  532.5 5.0 collective-permute-start.20
  538.3 6.7 %collective-permute-start.21 = (f32[512,128]{1,0:T(8,128)}, f32[512,128]{1,0:T(8,128)}, u32[]{:S(2)}, u32[]{:S(2)}) collective-permute-start(f32[512,128]{1,0:T(8,128)} %maximum_select_fusion.9), channel_id=1, source_target_pairs={{0,4},{4,0},{8,12},{12,8},{16,20},{20,16},{24,28},{28,24},{1,5},{5... | collective-permute-start | bytes 786440 | tf_op jit(solution)/shard_map/ppermute | solution.py:20
  (15 other events, 153.2 us)
Sparse Core Ops, SparseCore 0:
  46.0 23.7 all-gather.6
  116.6 33.5 all-gather.8
  222.1 57.3 all-gather.10
  315.5 51.3 all-reduce.4
  404.2 36.4 all-reduce.6
  476.2 33.6 all-reduce.8
  547.9 31.7 all-reduce.10
